TPU v7x, 32 devices: a whole 2x2x4 slice. The times are simulated.
32 devices in a mesh: layer: 4 (over y, x), row: 4 (over z), col: 2 (over core).
Axes of the slice: x: 2, y: 2, z: 4, core: 2. Of those that a mesh axis runs over, the one named last changes fastest.
Arguments:
- statistic: float32 [8, 7168, 7168], P('layer', 'row', 'col'), as said below
- eigenbasis: float32 [8, 7168, 1024], P('layer', 'col'), may hold values from -0.0625 to 0.0625
Outputs:
- refreshed: float32 [8, 7168, 1024], P('layer', ('row', 'col'))
Inputs may be any that keep to these rules, and one draw needn't show every extreme that they name: `statistic`: each layer's matrix is symmetric and positive definite.
All inputs are finite; a program needn't handle non-finite values.
Results may differ from a plain program's by a relative error of at most 0.00014.
Values sent between devices are 32-bit elements; how exact they have to be, the bound alone decides.
A program may use at most 192 MiB of HBM per device.

v0:
```python
import jax
import jax.numpy as jnp
from jax import lax
from jax.sharding import PartitionSpec as P


def contract(left_operand, right_operand):
    return lax.dot_general(
        left_operand,
        right_operand,
        (((0,), (0,)), ((), ())),
        precision=lax.Precision.HIGHEST,
        preferred_element_type=jnp.float32,
    )


def multiply(left_operand, right_operand):
    return jnp.dot(
        left_operand,
        right_operand,
        precision=lax.Precision.HIGHEST,
        preferred_element_type=jnp.float32,
    )


def on_device(statistic, eigenbasis):
    results = []
    for member in range(statistic.shape[0]):
        stat_layer = statistic[member]
        basis_layer = eigenbasis[member]
        row_product = lax.psum_scatter(
            multiply(stat_layer, basis_layer), "col", scatter_dimension=0, tiled=True
        )
        gram_matrix = lax.psum(contract(row_product, row_product), ("row", "col"))
        factor = jnp.linalg.cholesky(gram_matrix)
        result = lax.linalg.triangular_solve(
            factor, row_product, left_side=False, lower=True, transpose_a=True
        )
        results.append(result)
    return jnp.stack(results)


def solution(mesh):
    placed = (P("layer", "row", "col"), P("layer", "col", None))
    return jax.shard_map(
        on_device,
        mesh=mesh,
        in_specs=placed,
        out_specs=P("layer", ("row", "col"), None),
        check_vma=False,
    )
```

profile of v0, /device:TPU:0, one launch (start us, length us, event | category | flops | bytes accessed | tf_op | source)
XLA Modules:
  0.0 1133.4 jit_solution(6855643901012336946)
XLA Ops:
  6.5 89.5 %fusion.2 = f32[1792,1024]{1,0:T(8,128)} fusion(f32[2,1792,3584]{2,1,0:T(8,128)} %param.5, f32[2,3584,1024]{2,1,0:T(8,128)} %param.6), kind=kOutput, calls=%fused_computation.6 | convolution fusion | flops 78920024064 | bytes 47710208 | tf_op jit(solution)/shard_map/dot_general | solution.py:18
  96.3 89.6 %fusion = f32[1792,1024]{1,0:T(8,128)} fusion(f32[2,1792,3584]{2,1,0:T(8,128)} %param.5, f32[2,3584,1024]{2,1,0:T(8,128)} %param.6), kind=kOutput, calls=%fused_computation.4 | convolution fusion | flops 78920024064 | bytes 47710208 | tf_op jit(solution)/shard_map/dot_general | solution.py:18
  186.4 17.5 %fusion.150 = f32[1024,1024]{0,1:T(8,128)} fusion(f32[896,1024]{1,0:T(8,128)} %reduce-scatter.3.cloned.1.call-done), kind=kOutput, calls=%fused_computation.321 | convolution fusion | flops 11274289152 | bytes 7864320 | tf_op jit(solution)/shard_map/dot_general | solution.py:8
  204.9 17.5 %fusion.151 = f32[1024,1024]{0,1:T(8,128)} fusion(f32[896,1024]{1,0:T(8,128)} %reduce-scatter.5.cloned.1.call-done), kind=kOutput, calls=%fused_computation.322 | convolution fusion | flops 11274289152 | bytes 7864320 | tf_op jit(solution)/shard_map/dot_general | solution.py:8
  222.4 177.4 %all-reduce.4.cloned.1.call-done = (f32[1024,1024]{0,1:T(8,128)}, f32[1024,1024]{0,1:T(8,128)}) async-done(((f32[1024,1024]{0,1:T(8,128)}, f32[1024,1024]{0,1:T(8,128)}), (f32[1024,1024]{0,1:T(8,128)}, f32[1024,1024]{0,1:T(8,128)})) %all-reduce.4.cloned.1.call-update) | async-done | bytes 8388624 | tf_op jit(solution)/shard_map/psum | solution.py:34
  423.0 11.7 %cholesky.619 = f32[128,128]{1,0:T(8,128)S(1)} custom-call(f32[128,128]{1,0:T(8,128)S(1)} %cholesky.911), custom_call_target="Cholesky" | custom-call | tf_op jit(solution)/shard_map/jit(cholesky)/cholesky | solution.py:35
  451.0 11.9 %cholesky.638 = f32[128,128]{1,0:T(8,128)S(1)} custom-call(f32[128,128]{1,0:T(8,128)S(1)} %cholesky.915), custom_call_target="Cholesky" | custom-call | tf_op jit(solution)/shard_map/jit(cholesky)/cholesky | solution.py:35
  478.0 11.7 %cholesky.659 = f32[128,128]{1,0:T(8,128)S(1)} custom-call(f32[128,128]{1,0:T(8,128)S(1)} %cholesky.920), custom_call_target="Cholesky" | custom-call | tf_op jit(solution)/shard_map/jit(cholesky)/cholesky | solution.py:35
  504.7 11.7 %cholesky.678 = f32[128,128]{1,0:T(8,128)S(1)} custom-call(f32[128,128]{1,0:T(8,128)S(1)} %cholesky.925), custom_call_target="Cholesky" | custom-call | tf_op jit(solution)/shard_map/jit(cholesky)/cholesky | solution.py:35
  531.0 11.7 %cholesky.697 = f32[128,128]{1,0:T(8,128)S(1)} custom-call(f32[128,128]{1,0:T(8,128)S(1)} %cholesky.930), custom_call_target="Cholesky" | custom-call | tf_op jit(solution)/shard_map/jit(cholesky)/cholesky | solution.py:35
  557.2 11.7 %cholesky.716 = f32[128,128]{1,0:T(8,128)S(1)} custom-call(f32[128,128]{1,0:T(8,128)S(1)} %cholesky.935), custom_call_target="Cholesky" | custom-call | tf_op jit(solution)/shard_map/jit(cholesky)/cholesky | solution.py:35
  583.1 11.9 %cholesky.735 = f32[128,128]{1,0:T(8,128)S(1)} custom-call(f32[128,128]{1,0:T(8,128)S(1)} %cholesky.940), custom_call_target="Cholesky" | custom-call | tf_op jit(solution)/shard_map/jit(cholesky)/cholesky | solution.py:35
  608.8 11.7 %cholesky.752 = f32[128,128]{1,0:T(8,128)S(1)} custom-call(f32[128,128]{1,0:T(8,128)S(1)} %convolution_subtract_fusion.23), custom_call_target="Cholesky" | custom-call | tf_op jit(solution)/shard_map/jit(cholesky)/cholesky | solution.py:35
  631.5 22.8 %while.4 = (s32[]{:T(128)}, f32[1024,1024]{1,0:T(8,128)}, s32[8,2]{0,1:T(2,128)S(1)}, f32[8,128,128]{2,1,0:T(8,128)S(1)}, s32[]{:T(128)}) while((s32[]{:T(128)}, f32[1024,1024]{1,0:T(8,128)}, s32[8,2]{0,1:T(2,128)S(1)}, f32[8,128,128]{2,1,0:T(8,128)S(1)}, s32[]{:T(128)}) %tuple.114), condition=%wide.while_cond, body=%wide.while_body.sunk | while | flops 2 | bytes 131181 | solution.py:36
  654.3 79.0 %custom-call.62 = f32[8,128,128]{1,2,0:T(8,128)S(1)} custom-call(f32[8,128,128]{2,1,0:T(8,128)S(1)} %get-tuple-element.21), custom_call_target="InvertDiagBlocksLowerTriangular" | custom-call | tf_op jit(solution)/shard_map/triangular_solve/custom-call.7 | solution.py:36
  762.2 11.7 %cholesky.786 = f32[128,128]{1,0:T(8,128)S(1)} custom-call(f32[128,128]{1,0:T(8,128)S(1)} %cholesky.948), custom_call_target="Cholesky" | custom-call | tf_op jit(solution)/shard_map/jit(cholesky)/cholesky | solution.py:35
  789.1 11.7 %cholesky.807 = f32[128,128]{1,0:T(8,128)S(1)} custom-call(f32[128,128]{1,0:T(8,128)S(1)} %cholesky.953), custom_call_target="Cholesky" | custom-call | tf_op jit(solution)/shard_map/jit(cholesky)/cholesky | solution.py:35
  815.4 11.9 %cholesky.826 = f32[128,128]{1,0:T(8,128)S(1)} custom-call(f32[128,128]{1,0:T(8,128)S(1)} %cholesky.958), custom_call_target="Cholesky" | custom-call | tf_op jit(solution)/shard_map/jit(cholesky)/cholesky | solution.py:35
  841.9 11.7 %cholesky.845 = f32[128,128]{1,0:T(8,128)S(1)} custom-call(f32[128,128]{1,0:T(8,128)S(1)} %cholesky.963), custom_call_target="Cholesky" | custom-call | tf_op jit(solution)/shard_map/jit(cholesky)/cholesky | solution.py:35
  868.4 11.7 %cholesky.864 = f32[128,128]{1,0:T(8,128)S(1)} custom-call(f32[128,128]{1,0:T(8,128)S(1)} %cholesky.968), custom_call_target="Cholesky" | custom-call | tf_op jit(solution)/shard_map/jit(cholesky)/cholesky | solution.py:35
  894.3 11.7 %cholesky.883 = f32[128,128]{1,0:T(8,128)S(1)} custom-call(f32[128,128]{1,0:T(8,128)S(1)} %cholesky.973), custom_call_target="Cholesky" | custom-call | tf_op jit(solution)/shard_map/jit(cholesky)/cholesky | solution.py:35
  919.9 11.7 %cholesky.900 = f32[128,128]{1,0:T(8,128)S(1)} custom-call(f32[128,128]{1,0:T(8,128)S(1)} %convolution_subtract_fusion.22), custom_call_target="Cholesky" | custom-call | tf_op jit(solution)/shard_map/jit(cholesky)/cholesky | solution.py:35
  942.7 22.8 %while.5 = (s32[]{:T(128)}, f32[1024,1024]{1,0:T(8,128)}, s32[8,2]{0,1:T(2,128)S(1)}, f32[8,128,128]{2,1,0:T(8,128)S(1)}, s32[]{:T(128)}) while((s32[]{:T(128)}, f32[1024,1024]{1,0:T(8,128)}, s32[8,2]{0,1:T(2,128)S(1)}, f32[8,128,128]{2,1,0:T(8,128)S(1)}, s32[]{:T(128)}) %tuple.124), condition=%wide.while_cond.clone, body=%wide.while_body.clone.sunk | while | flops 2 | bytes 131181 | solution.py:36
  965.5 78.8 %custom-call.70 = f32[8,128,128]{1,2,0:T(8,128)S(1)} custom-call(f32[8,128,128]{2,1,0:T(8,128)S(1)} %get-tuple-element.22), custom_call_target="InvertDiagBlocksLowerTriangular" | custom-call | tf_op jit(solution)/shard_map/triangular_solve/custom-call.7 | solution.py:36
  (194 shorter events, 383.6 us)
Async XLA Ops:
  6.5 179.8 %reduce-scatter.3.cloned.1.call-start = ((), (), s32[]{:S(2)}) async-start(), calls=%async_computation.2 | async-start | bytes 11010048 | tf_op jit(solution)/shard_map/reduce_scatter | solution.py:31
  96.1 108.8 %reduce-scatter.5.cloned.1.call-start = ((), (), s32[]{:S(2)}) async-start(), calls=%async_computation.3 | async-start | bytes 11010048 | tf_op jit(solution)/shard_map/reduce_scatter | solution.py:31
  185.9 213.9 %all-reduce.4.cloned.1.call-start = ((), (), s32[]{:S(2)}) async-start(), calls=%async_computation.4 | async-start | bytes 16777216 | tf_op jit(solution)/shard_map/psum | solution.py:34
  421.1 1.9 copy-start
  1044.4 4.6 copy-start.2
  1072.5 8.1 copy-start.1
Sparse Core Ops, SparseCore 0:
  96.2 18.8 reduce-scatter.2
  186.0 18.8 reduce-scatter.4
  222.5 177.2 all-reduce.3
where the time goes:
time: 1140 us; the launch traced here: 1130 us
  other arithmetic  526 us (46%)
  matrix products  331 us (29%)
  waiting for transfers between devices  178 us (16%)
  local copies, waits for them, and re-layouts  72.2 us (6%)
  between operations  23.9 us (2%)
    another operation x62, other arithmetic, on_device(): factor = jnp.linalg.cholesky(gram_matrix)  345 us
    dot_general x2, matrix products, multiply(): jnp.dot(left_operand, right_operand, precision=lax.Precision.HIGHEST, pre...  179 us
    psum x1, waiting for transfers between devices, on_device(): gram_matrix = lax.psum(contract(row_product, row_product), ('row', 'col'))  177 us
    another operation x5, other arithmetic, on_device(): lax.linalg.triangular_solve(factor, row_product, left_side=False, lower=T...  167 us
    another operation x30, matrix products, on_device(): lax.linalg.triangular_solve(factor, row_product, left_side=False, lower=T...  70.3 us
    another operation x28, matrix products, on_device(): factor = jnp.linalg.cholesky(gram_matrix)  47 us
    another operation x51, local copies, waits for them, and re-layouts, on_device(): lax.linalg.triangular_solve(factor, row_product, left_side=False, lower=T...  45.5 us
    dot_general x2, matrix products, contract(): lax.dot_general(left_operand, right_operand, (((0,), (0,)), ((), ())), pr...  35 us
  transfers between devices with their start and end apart: 3, of which 2 were waited for; matrix products, arithmetic and copies ran while one was open for 9% of the time, Pallas kernels for 0%

commit v1 on v0

--- a/solution.py
+++ b/solution.py
@@ -31,7 +31,9 @@
         row_product = lax.psum_scatter(
             multiply(stat_layer, basis_layer), "col", scatter_dimension=0, tiled=True
         )
-        gram_matrix = lax.psum(contract(row_product, row_product), ("row", "col"))
+        gram_matrix = jnp.sum(
+            lax.all_gather(contract(row_product, row_product), ("row", "col")), axis=0
+        )
         factor = jnp.linalg.cholesky(gram_matrix)
         result = lax.linalg.triangular_solve(
             factor, row_product, left_side=False, lower=True, transpose_a=True

time: 1140 us -> 1270 us (1.11)
  waiting for transfers between devices: 178 us -> 275 us
  other arithmetic: 526 us -> 556 us
    all_gather x0 -> x2, waiting for transfers between devices: none -> 274 us  [on_device(): lax.all_gather(contract(row_product, row_product), ('row', 'col'))]
    psum x1 -> x0, waiting for transfers between devices: 177 us -> none  [on_device(): gram_matrix = lax.psum(contract(row_product, row_product), ('row', 'col'))]
    reduce_sum x0 -> x2, other arithmetic: none -> 31.8 us  [on_device(): jnp.sum(lax.all_gather(contract(row_product, row_product), ('row', 'col')...]
    another operation x62 -> x60, other arithmetic: 345 us -> 345 us  [on_device(): factor = jnp.linalg.cholesky(gram_matrix)]
  transfers between devices with their start and end apart: 3 -> 4, of which waited for: 2 -> 2; matrix products, arithmetic and copies ran while one was open for 9% -> 36% of each run, Pallas kernels for 0% -> 0%
where the time goes in v1:
time: 1270 us; the launch traced here: 1260 us
  other arithmetic  556 us (44%)
  matrix products  330 us (26%)
  waiting for transfers between devices  275 us (22%)
  local copies, waits for them, and re-layouts  74.2 us (6%)
  between operations  24.5 us (2%)
    another operation x60, other arithmetic, on_device(): factor = jnp.linalg.cholesky(gram_matrix)  345 us
    all_gather x2, waiting for transfers between devices, on_device(): lax.all_gather(contract(row_product, row_product), ('row', 'col'))  274 us
    dot_general x2, matrix products, multiply(): jnp.dot(left_operand, right_operand, precision=lax.Precision.HIGHEST, pre...  179 us
    another operation x5, other arithmetic, on_device(): lax.linalg.triangular_solve(factor, row_product, left_side=False, lower=T...  167 us
    another operation x30, matrix products, on_device(): lax.linalg.triangular_solve(factor, row_product, left_side=False, lower=T...  70.3 us
    another operation x28, matrix products, on_device(): factor = jnp.linalg.cholesky(gram_matrix)  46.2 us
    another operation x51, local copies, waits for them, and re-layouts, on_device(): lax.linalg.triangular_solve(factor, row_product, left_side=False, lower=T...  45.7 us
    dot_general x2, matrix products, contract(): lax.dot_general(left_operand, right_operand, (((0,), (0,)), ((), ())), pr...  34.7 us
  transfers between devices with their start and end apart: 4, of which 2 were waited for; matrix products, arithmetic and copies ran while one was open for 36% of the time, Pallas kernels for 0%

profile of v1, /device:TPU:0, one launch (start us, length us, event | category | flops | bytes accessed | tf_op | source)
XLA Modules:
  0.0 1261.7 jit_solution(4295637773725847179)
XLA Ops:
  6.5 89.5 %fusion.2 = f32[1792,1024]{1,0:T(8,128)} fusion(f32[2,1792,3584]{2,1,0:T(8,128)} %param.5, f32[2,3584,1024]{2,1,0:T(8,128)} %param.6), kind=kOutput, calls=%fused_computation.6 | convolution fusion | flops 78920024064 | bytes 47710208 | tf_op jit(solution)/shard_map/dot_general | solution.py:18
  96.3 89.6 %fusion = f32[1792,1024]{1,0:T(8,128)} fusion(f32[2,1792,3584]{2,1,0:T(8,128)} %param.5, f32[2,3584,1024]{2,1,0:T(8,128)} %param.6), kind=kOutput, calls=%fused_computation.4 | convolution fusion | flops 78920024064 | bytes 47710208 | tf_op jit(solution)/shard_map/dot_general | solution.py:18
  186.4 17.4 %fusion.150 = f32[1024,1024]{1,0:T(8,128)} fusion(f32[896,1024]{1,0:T(8,128)} %reduce-scatter.3.cloned.1.call-done), kind=kOutput, calls=%fused_computation.321 | convolution fusion | flops 11274289152 | bytes 7864320 | tf_op jit(solution)/shard_map/dot_general | solution.py:8
  204.9 17.3 %fusion.151 = f32[1024,1024]{1,0:T(8,128)} fusion(f32[896,1024]{1,0:T(8,128)} %reduce-scatter.5.cloned.1.call-done), kind=kOutput, calls=%fused_computation.322 | convolution fusion | flops 11274289152 | bytes 7864320 | tf_op jit(solution)/shard_map/dot_general | solution.py:8
  222.3 274.2 %all-gather.5.cloned.1.call-done = f32[8192,1024]{1,0:T(8,128)} async-done(((f32[1024,1024]{1,0:T(8,128)}), f32[8192,1024]{1,0:T(8,128)}) %all-gather.5.cloned.1.call-update) | async-done | bytes 33554448 | tf_op jit(solution)/shard_map/all_gather | solution.py:35
  496.4 17.2 %reduce_sum.18 = f32[1024,1024]{1,0:T(8,128)} reduce(f32[8,1024,1024]{2,1,0:T(8,128)} %bitcast.245, f32[]{:T(128)} %constant.194.clone.1), dimensions={0}, to_apply=%region_1.0 | reduce | flops 7340032 | bytes 37748740 | tf_op jit(solution)/shard_map/reduce_sum | solution.py:34
  525.8 11.7 cholesky.619
  553.7 11.9 cholesky.638
  579.4 11.7 cholesky.659
  605.2 12.1 cholesky.678
  631.2 11.7 cholesky.697
  656.9 11.7 cholesky.716
  682.2 11.7 cholesky.735
  707.0 11.7 cholesky.752
  734.6 22.4 %while.4 = (s32[]{:T(128)}, f32[1024,1024]{1,0:T(8,128)}, s32[8,2]{0,1:T(2,128)S(1)}, f32[8,128,128]{2,1,0:T(8,128)S(1)}, s32[]{:T(128)}) while((s32[]{:T(128)}, f32[1024,1024]{1,0:T(8,128)}, s32[8,2]{0,1:T(2,128)S(1)}, f32[8,128,128]{2,1,0:T(8,128)S(1)}, s32[]{:T(128)}) %tuple.115), condition=%wide.while_cond, body=%wide.while_body.sunk | while | flops 2 | bytes 131181 | solution.py:38
  757.0 78.6 %custom-call.62 = f32[8,128,128]{1,2,0:T(8,128)S(1)} custom-call(f32[8,128,128]{2,1,0:T(8,128)S(1)} %get-tuple-element.21), custom_call_target="InvertDiagBlocksLowerTriangular" | custom-call | tf_op jit(solution)/shard_map/triangular_solve/custom-call.7 | solution.py:38
  835.7 14.7 %reduce_sum.19 = f32[1024,1024]{1,0:T(8,128)} reduce(f32[8,1024,1024]{2,1,0:T(8,128)} %bitcast.244, f32[]{:T(128)} %constant.194.clone.1), dimensions={0}, to_apply=%region_19.22 | reduce | flops 7340032 | bytes 37748740 | tf_op jit(solution)/shard_map/reduce_sum | solution.py:34
  862.5 11.7 cholesky.767
  890.4 11.9 cholesky.786
  916.1 11.7 cholesky.807
  942.4 11.9 cholesky.826
  1021.2 11.9 cholesky.883
  1070.4 23.5 %while.5 = (s32[]{:T(128)}, f32[1024,1024]{1,0:T(8,128)}, s32[8,2]{0,1:T(2,128)S(1)}, f32[8,128,128]{2,1,0:T(8,128)S(1)}, s32[]{:T(128)}) while((s32[]{:T(128)}, f32[1024,1024]{1,0:T(8,128)}, s32[8,2]{0,1:T(2,128)S(1)}, f32[8,128,128]{2,1,0:T(8,128)S(1)}, s32[]{:T(128)}) %tuple.126), condition=%wide.while_cond.clone, body=%wide.while_body.clone.sunk | while | flops 2 | bytes 131181 | solution.py:38
  1093.8 78.8 %custom-call.70 = f32[8,128,128]{1,2,0:T(8,128)S(1)} custom-call(f32[8,128,128]{2,1,0:T(8,128)S(1)} %get-tuple-element.22), custom_call_target="InvertDiagBlocksLowerTriangular" | custom-call | tf_op jit(solution)/shard_map/triangular_solve/custom-call.7 | solution.py:38
  (200 shorter events, 406.4 us)
Async XLA Ops:
  6.5 179.8 %reduce-scatter.3.cloned.1.call-start = ((), (), s32[]{:S(2)}) async-start(), calls=%async_computation.2 | async-start | bytes 11010048 | tf_op jit(solution)/shard_map/reduce_scatter | solution.py:31
  96.1 108.8 %reduce-scatter.5.cloned.1.call-start = ((), (), s32[]{:S(2)}) async-start(), calls=%async_computation.3 | async-start | bytes 11010048 | tf_op jit(solution)/shard_map/reduce_scatter | solution.py:31
  185.9 310.5 %all-gather.5.cloned.1.call-start = ((), (), s32[]{:S(2)}) async-start(), calls=%async_computation.4 | async-start | bytes 37748736 | tf_op jit(solution)/shard_map/all_gather | solution.py:35
  203.8 631.9 %all-gather.7.cloned.1.call-start = ((), (), s32[]{:S(2)}) async-start(), calls=%async_computation.5 | async-start | bytes 37748736 | tf_op jit(solution)/shard_map/all_gather | solution.py:35
  523.7 2.0 copy-start.1
  860.5 1.9 copy-start
  1172.7 4.6 copy-start.3
  1200.8 8.1 copy-start.2
Sparse Core Ops, SparseCore 0:
  96.2 18.8 reduce-scatter.2
  186.0 18.8 reduce-scatter.4
  206.5 289.8 all-gather.4
  497.9 286.7 all-gather.6
